TPU v7x, 32 devices: a whole 2x2x4 slice. The times are simulated.
32 devices in a mesh: tok: 16 (over z, y, x), hd: 2 (over core).
Axes of the slice: x: 2, y: 2, z: 4, core: 2. Of those that a mesh axis runs over, the one named last changes fastest.
Arguments:
- hidden_in: bfloat16 [16384, 768], P(('tok', 'hd')), may hold values from -6 to 6
- norm_gains: bfloat16 [2, 768], P(None, ('tok', 'hd')), may hold values from 0.099609375 to 1.8984375
- w_qkv: bfloat16 [2304, 768], P(('tok', 'hd')), may hold values from -0.21875 to 0.21875
- w_attn_out: bfloat16 [768, 768], P(('tok', 'hd')), may hold values from -1.75 to 1.75
- w_in: bfloat16 [2304, 768], P(('tok', 'hd')), may hold values from -0.21875 to 0.21875
- w_down: bfloat16 [768, 1152], P(('tok', 'hd')), may hold values from -0.1875 to 0.1875
- cotangent: bfloat16 [16384, 768], P(('tok', 'hd')), may hold values from -6 to 6
- segment_ids: int32 [16384], P(('tok', 'hd')), may hold values from 0 to 31, as said below
- row_counts: int32 [32], P(('tok', 'hd')), may hold values from 256 to 512, as said below
Outputs:
- output: bfloat16 [16384, 768], P(('tok', 'hd'))
- input_grad: bfloat16 [16384, 768], P(('tok', 'hd'))
- grad_qkv: float32 [2304, 768], P(('tok', 'hd'))
- grad_attn_out: float32 [768, 768], P(('tok', 'hd'))
- grad_in: float32 [2304, 768], P(('tok', 'hd'))
- grad_down: float32 [768, 1152], P(('tok', 'hd'))
- grad_gains: float32 [2, 768], P(None, ('tok', 'hd'))
Inputs may be any that keep to these rules, and one draw needn't show every extreme that they name: `segment_ids`: within each group of 1024 rows the ids start at 0 and never fall; a document is a run of rows with one id; documents begin only at rows whose index within the group is a multiple of 32, and always at rows whose index within a block is 256, so a document may span two blocks of a group. In every draw some group holds 32 documents. `row_counts`: rows of a block at or beyond its count are padding.
All inputs are finite; a program needn't handle non-finite values.
Results may differ from a plain program's by a relative error of at most 0.015.
Values may be sent and summed in bfloat16 or wider, within the bound.
A program may use at most 192 MiB of HBM per device.

v0:
```python
import math
import jax
import jax.numpy as jnp
from jax import lax
from jax.sharding import PartitionSpec as P

HEADS = 12
HEAD_DIM = 64
EPS = 1e-05
THETA = 160000.0
NEG = -1e30


def layer_norm(row_values, gain):
    mean_value = jnp.mean(row_values, axis=-1, keepdims=True)
    centred = row_values - mean_value
    variance = jnp.mean(centred * centred, axis=-1, keepdims=True)
    return centred * lax.rsqrt(variance + EPS) * gain


def doc_positions(seg_ids):
    row_index = jnp.arange(seg_ids.shape[0], dtype=jnp.int32)
    begins = jnp.concatenate([jnp.ones((1,), dtype=jnp.bool_), seg_ids[1:] != seg_ids[:-1]])
    first_row = lax.cummax(jnp.where(begins, row_index, 0), axis=0)
    return (row_index - first_row).astype(jnp.float32)


def rotary_tables(position, head_size):
    half_size = head_size // 2
    freqs = THETA ** (-jnp.arange(half_size, dtype=jnp.float32) * 2.0 / head_size)
    angles = position[:, None] * freqs[None, :]
    angles = jnp.concatenate([angles, angles], axis=1)
    return (jnp.cos(angles), jnp.sin(angles))


def rotate(head_values, cos_table, sin_table):
    half_size = head_values.shape[-1] // 2
    turned = jnp.concatenate([-head_values[..., half_size:], head_values[..., :half_size]], axis=-1)
    return head_values * cos_table[:, None, :] + turned * sin_table[:, None, :]


def times_t(left, right):
    return lax.dot_general(
        left, right, (((1,), (1,)), ((), ())), preferred_element_type=jnp.float32
    )


def outer_sum(left, right):
    return lax.dot_general(
        left, right, (((0,), (0,)), ((), ())), preferred_element_type=jnp.float32
    )


def times(left, right):
    return jnp.dot(left, right, preferred_element_type=jnp.float32)


def gated(gate, up_part):
    return jax.nn.gelu(gate, approximate=False) * up_part


def block_scores(queries, keys, seg_ids, ok_rows, first_row, block_size):
    query_block = lax.dynamic_slice_in_dim(queries, first_row, block_size, 0)
    seg_query = lax.dynamic_slice_in_dim(seg_ids, first_row, block_size, 0)
    ok_query = lax.dynamic_slice_in_dim(ok_rows, first_row, block_size, 0)
    query_index = first_row + jnp.arange(block_size, dtype=jnp.int32)
    key_index = jnp.arange(seg_ids.shape[0], dtype=jnp.int32)
    same_doc = (seg_query[:, None] == seg_ids[None, :]) & ok_query[:, None] & ok_rows[None, :]
    allowed = same_doc | (query_index[:, None] == key_index[None, :])
    scores = (
        jnp.einsum("qhd,khd->hqk", query_block, keys, preferred_element_type=jnp.float32) * 0.125
    )
    return (query_block, allowed, jnp.where(allowed[None], scores, NEG))


def attend_forward(queries, keys, values, seg_ids, ok_rows, block_size):

    def one_block(block_index):
        first_row = block_index * block_size
        _, _, masked = block_scores(queries, keys, seg_ids, ok_rows, first_row, block_size)
        top_score = jnp.max(masked, axis=-1, keepdims=True)
        weights_exp = jnp.exp(masked - top_score)
        total = jnp.sum(weights_exp, axis=-1, keepdims=True)
        probs = (weights_exp / total).astype(jnp.bfloat16)
        mixed = jnp.einsum("hqk,khd->qhd", probs, values, preferred_element_type=jnp.float32)
        return (mixed.astype(jnp.bfloat16), (top_score + jnp.log(total))[..., 0])

    block_ids = jnp.arange(queries.shape[0] // block_size, dtype=jnp.int32)
    mixed, log_totals = lax.map(one_block, block_ids)
    return (mixed.reshape(queries.shape), log_totals)


def attend_backward(queries, keys, values, grad_mixed, log_totals, seg_ids, ok_rows, block_size):

    def one_block(carry, inputs_here):
        grad_keys, grad_values = carry
        block_index, log_total = inputs_here
        first_row = block_index * block_size
        query_block, allowed, masked = block_scores(
            queries, keys, seg_ids, ok_rows, first_row, block_size
        )
        probs = jnp.exp(masked - log_total[..., None])
        probs_low = probs.astype(jnp.bfloat16)
        grad_block = lax.dynamic_slice_in_dim(grad_mixed, first_row, block_size, 0)
        grad_probs = jnp.einsum(
            "qhd,khd->hqk", grad_block, values, preferred_element_type=jnp.float32
        )
        inner = jnp.sum(probs * grad_probs, axis=-1, keepdims=True)
        grad_scores = jnp.where(allowed[None], probs * (grad_probs - inner), 0.0).astype(
            jnp.bfloat16
        )
        grad_query = (
            jnp.einsum("hqk,khd->qhd", grad_scores, keys, preferred_element_type=jnp.float32)
            * 0.125
        )
        grad_keys = (
            grad_keys
            + jnp.einsum(
                "hqk,qhd->khd", grad_scores, query_block, preferred_element_type=jnp.float32
            )
            * 0.125
        )
        grad_values = grad_values + jnp.einsum(
            "hqk,qhd->khd", probs_low, grad_block, preferred_element_type=jnp.float32
        )
        return ((grad_keys, grad_values), grad_query.astype(jnp.bfloat16))

    zero_grads = jnp.zeros(keys.shape, jnp.float32)
    block_ids = jnp.arange(queries.shape[0] // block_size, dtype=jnp.int32)
    (grad_keys, grad_values), grad_query = lax.scan(
        one_block, (zero_grads, zero_grads), (block_ids, log_totals)
    )
    return (
        grad_query.reshape(queries.shape),
        grad_keys.astype(jnp.bfloat16),
        grad_values.astype(jnp.bfloat16),
    )


def per_device(
    hidden_in, norm_gains, w_qkv, w_attn_out, w_in, w_down, cotangent, segment_ids, row_counts
):
    row_total, width = hidden_in.shape
    group_count = lax.axis_size("hd")
    heads_here = HEADS // group_count
    part_width = width // group_count
    group_rows = group_count * row_total
    block_size = min(512, group_rows)
    ff_width = w_down.shape[1]
    gathered = (
        lax.all_gather(w_qkv, ("tok", "hd"), axis=0, tiled=True),
        lax.all_gather(w_attn_out, ("tok", "hd"), axis=0, tiled=True),
        lax.all_gather(w_in, ("tok", "hd"), axis=0, tiled=True),
        lax.all_gather(w_down, ("tok", "hd"), axis=0, tiled=True),
        lax.all_gather(norm_gains, ("tok", "hd"), axis=1, tiled=True),
    )
    full_qkv, full_attn_out, full_in, full_down, full_gains = gathered
    gain_attn = full_gains[0].astype(jnp.float32)
    gain_mlp = full_gains[1].astype(jnp.float32)
    row_index = jnp.arange(row_total, dtype=jnp.int32)
    keep_rows = (row_index < row_counts[0]).astype(jnp.float32)[:, None]
    seg_pair, count_pair = (
        lax.all_gather(segment_ids, "hd", axis=0, tiled=True),
        lax.all_gather(row_counts, "hd", axis=0, tiled=True),
    )
    ok_pair = jnp.concatenate([row_index < count_pair[anchor] for anchor in range(group_count)])
    group_positions = doc_positions(seg_pair)
    own_start = lax.axis_index("hd") * row_total
    own_positions = lax.dynamic_slice_in_dim(group_positions, own_start, row_total, 0)
    cos_table, sin_table = rotary_tables(own_positions, HEAD_DIM)
    wide_in = hidden_in.astype(jnp.float32)
    normed_f, attn_norm_pull = jax.vjp(layer_norm, wide_in, gain_attn)
    normed1 = normed_f.astype(jnp.bfloat16)
    qkv = times_t(normed1, full_qkv)
    q_rot = rotate(qkv[:, :width].reshape(row_total, HEADS, HEAD_DIM), cos_table, sin_table)
    k_rot = rotate(
        qkv[:, width : 2 * width].reshape(row_total, HEADS, HEAD_DIM), cos_table, sin_table
    )
    packed = jnp.concatenate(
        [q_rot.reshape(row_total, width), k_rot.reshape(row_total, width), qkv[:, 2 * width :]],
        axis=1,
    ).astype(jnp.bfloat16)
    packed = packed.reshape(row_total, 3, group_count, part_width)
    head_rows = lax.all_to_all(packed, "hd", split_axis=2, concat_axis=0, tiled=True)
    q_heads = head_rows[:, 0, 0].reshape(group_rows, heads_here, HEAD_DIM)
    k_heads = head_rows[:, 1, 0].reshape(group_rows, heads_here, HEAD_DIM)
    v_heads = head_rows[:, 2, 0].reshape(group_rows, heads_here, HEAD_DIM)
    mixed, log_totals = attend_forward(q_heads, k_heads, v_heads, seg_pair, ok_pair, block_size)
    mixed_heads = mixed.reshape(group_rows, 1, part_width)
    attended = lax.all_to_all(mixed_heads, "hd", split_axis=0, concat_axis=1, tiled=True).reshape(
        row_total, width
    )
    residual = wide_in + keep_rows * times_t(attended, full_attn_out)
    normed_g, mlp_norm_pull = jax.vjp(layer_norm, residual, gain_mlp)
    normed2 = normed_g.astype(jnp.bfloat16)
    both_parts = times_t(normed2, full_in)
    hidden_f, gate_pull = jax.vjp(gated, both_parts[:, :ff_width], both_parts[:, ff_width:])
    hidden = hidden_f.astype(jnp.bfloat16)
    output = (residual + keep_rows * times_t(hidden, full_down)).astype(jnp.bfloat16)
    back_weights = (
        lax.all_gather(w_qkv, ("tok", "hd"), axis=0, tiled=True),
        lax.all_gather(w_attn_out, ("tok", "hd"), axis=0, tiled=True),
        lax.all_gather(w_in, ("tok", "hd"), axis=0, tiled=True),
        lax.all_gather(w_down, ("tok", "hd"), axis=0, tiled=True),
        lax.all_gather(norm_gains, ("tok", "hd"), axis=1, tiled=True),
    )
    back_qkv, back_attn_out, back_in, back_down, _ = back_weights
    grad_out_rows = cotangent.astype(jnp.float32)
    grad_branch2 = (keep_rows * grad_out_rows).astype(jnp.bfloat16)
    down_term = outer_sum(grad_branch2, hidden)
    grad_hidden = times(grad_branch2, back_down)
    grad_gate, grad_up = gate_pull(grad_hidden)
    grad_both = jnp.concatenate([grad_gate, grad_up], axis=1).astype(jnp.bfloat16)
    in_term = outer_sum(grad_both, normed2)
    grad_normed2 = times(grad_both, back_in)
    grad_res_norm, gain_mlp_term = mlp_norm_pull(grad_normed2)
    grad_residual = grad_out_rows + grad_res_norm
    grad_branch1 = (keep_rows * grad_residual).astype(jnp.bfloat16)
    attn_out_term = outer_sum(grad_branch1, attended)
    grad_attended = times(grad_branch1, back_attn_out).astype(jnp.bfloat16)
    grad_heads = lax.all_to_all(
        grad_attended.reshape(row_total, group_count, part_width),
        "hd",
        split_axis=1,
        concat_axis=0,
        tiled=True,
    )
    grad_heads = grad_heads.reshape(group_rows, heads_here, HEAD_DIM)
    grad_query, grad_keys, grad_values = attend_backward(
        q_heads, k_heads, v_heads, grad_heads, log_totals, seg_pair, ok_pair, block_size
    )
    grad_stack = jnp.stack(
        [
            grad_query.reshape(group_rows, part_width),
            grad_keys.reshape(group_rows, part_width),
            grad_values.reshape(group_rows, part_width),
        ],
        axis=1,
    )
    grad_stack = grad_stack.reshape(group_rows, 3, 1, part_width)
    grad_rows = lax.all_to_all(grad_stack, "hd", split_axis=0, concat_axis=2, tiled=True).reshape(
        row_total, 3, width
    )
    grad_q = rotate(
        grad_rows[:, 0].astype(jnp.float32).reshape(row_total, HEADS, HEAD_DIM),
        cos_table,
        -sin_table,
    )
    grad_k = rotate(
        grad_rows[:, 1].astype(jnp.float32).reshape(row_total, HEADS, HEAD_DIM),
        cos_table,
        -sin_table,
    )
    grad_qkv = jnp.concatenate(
        [
            grad_q.reshape(row_total, width).astype(jnp.bfloat16),
            grad_k.reshape(row_total, width).astype(jnp.bfloat16),
            grad_rows[:, 2],
        ],
        axis=1,
    )
    qkv_term = outer_sum(grad_qkv, normed1)
    grad_normed1 = times(grad_qkv, back_qkv)
    grad_in_norm, gain_attn_term = attn_norm_pull(grad_normed1)
    input_grad = (grad_residual + grad_in_norm).astype(jnp.bfloat16)
    gain_terms = jnp.stack([gain_attn_term, gain_mlp_term])
    sum_qkv, sum_attn_out, sum_in, sum_down, sum_gains = (
        lax.psum_scatter(qkv_term, ("tok", "hd"), scatter_dimension=0, tiled=True),
        lax.psum_scatter(attn_out_term, ("tok", "hd"), scatter_dimension=0, tiled=True),
        lax.psum_scatter(in_term, ("tok", "hd"), scatter_dimension=0, tiled=True),
        lax.psum_scatter(down_term, ("tok", "hd"), scatter_dimension=0, tiled=True),
        lax.psum_scatter(gain_terms, ("tok", "hd"), scatter_dimension=1, tiled=True),
    )
    token_total = row_total * lax.axis_size("tok") * lax.axis_size("hd")
    scale = 1.0 / math.sqrt(token_total)
    return (
        output,
        input_grad,
        sum_qkv * scale,
        sum_attn_out * scale,
        sum_in * scale,
        sum_down * scale,
        sum_gains * scale,
    )


def solution(mesh):
    return jax.shard_map(
        per_device,
        mesh=mesh,
        in_specs=(
            P(("tok", "hd"), None),
            P(None, ("tok", "hd")),
            P(("tok", "hd"), None),
            P(("tok", "hd"), None),
            P(("tok", "hd"), None),
            P(("tok", "hd"), None),
            P(("tok", "hd"), None),
            P(("tok", "hd")),
            P(("tok", "hd")),
        ),
        out_specs=(
            P(("tok", "hd"), None),
            P(("tok", "hd"), None),
            P(("tok", "hd"), None),
            P(("tok", "hd"), None),
            P(("tok", "hd"), None),
            P(("tok", "hd"), None),
            P(None, ("tok", "hd")),
        ),
        check_vma=False,
    )
```

profile of v0, /device:TPU:0, one launch (start us, length us, event | category | flops | bytes accessed | tf_op | source)
XLA Modules:
  0.0 732.9 jit_solution(1573320555635671999)
XLA Ops:
  21.4 43.4 %all-gather.1 = bf16[32,24,2]{1,2,0:T(2,128)(2,1)S(1)} all-gather(bf16[1,24,2]{1,2,0:T(2,128)(2,1)} %bitcast.176), channel_id=1, replica_groups=mesh['tok'=16,'hd'=2] {'tok','hd'}, dimensions={0}, use_global_device_ids=true | all-gather | bytes 3168 | tf_op jit(solution)/shard_map/all_gather | solution.py:155
  73.7 4.1 fusion.125
  98.8 4.2 add_convert_fusion.4
  105.9 5.8 all_to_all.63
  113.1 25.3 %while.27 = (s32[]{:T(128)}, bf16[2,512,6,64]{1,3,2,0:T(8,128)(2,1)S(1)}, f32[2,6,512]{2,1,0:T(8,128)S(1)}, s32[2]{0:T(128)S(1)}, s32[1024]{0:T(1024)S(1)}, /*in...) while((s32[]{:T(128)}, ...), condition=%wide.region_7.8_spmd, body=%wide.region_4.7_spmd.sunk | while | flops 845870592 | bytes 42341076 | solution.py:89
  121.3 4.4 fusion.180
  130.3 3.6 fusion.179
  133.9 4.4 fusion.180
  147.5 5.8 all_to_all.64
  163.8 27.4 %all-gather.11.cloned.1.call-done = bf16[2304,768]{1,0:T(8,128)(2,1)} async-done(((bf16[72,768]{1,0:T(8,128)(2,1)}), bf16[2304,768]{1,0:T(8,128)(2,1)}) %all-gather.11.cloned.1.call-update) | async-done | bytes 3538960 | tf_op jit(solution)/shard_map/all_gather | solution.py:153
  191.2 6.8 fusion.128
  197.9 50.2 %all-gather.13.cloned.1.call-done = bf16[768,1152]{1,0:T(8,128)(2,1)} async-done(((bf16[24,1152]{1,0:T(8,128)(2,1)}), bf16[768,1152]{1,0:T(8,128)(2,1)}) %all-gather.13.cloned.1.call-update) | async-done | bytes 1769488 | tf_op jit(solution)/shard_map/all_gather | solution.py:154
  248.1 9.0 %add_convert_fusion = (bf16[512,1152]{1,0:T(8,128)(2,1)S(1)}, f32[512,1152]{1,0:T(8,128)S(1)}, f32[512,1152]{1,0:T(8,128)S(1)}) fusion(f32[512,2304]{1,0:T(8,128)} %fusion.128, bf16[768,1152]{1,0:T(8,128)(2,1)} %all-gather.13.cloned.1.call-done, bf16[512,768]{1,0:T(8,128)(2,1)S(1)} %copy-done.8, f32[512]{0:T(512)S(1)} %copy-done.32), kind=kOutput, calls=%fused_computation.82 | convolution fusion | flops 950206464 | bytes 13174784 | tf_op jit(solution)/shard_map/dot_general | solution.py:55
  268.9 4.3 fusion.107
  273.3 7.2 fusion.103
  283.8 4.4 all_to_all.65
  294.3 145.9 %while.28 = (s32[]{:T(128)}, f32[1024,6,64]{0,2,1:T(8,128)}, f32[1024,6,64]{0,2,1:T(8,128)}, bf16[2,512,6,64]{1,3,2,0:T(8,128)(2,1)}, s32[2]{0:T(128)S(1)}, /*in...) while((s32[]{:T(128)}, f32[1024,6,64]{0,2,1:T(8,128)}, ...), condition=%wide.region_14.15_spmd.clone, body=%wide.region_12.14_spmd.clone.sunk | while | flops 2100044288 | bytes 205775664 | solution.py:130
  298.3 5.0 bitcast_add_fusion.7
  303.3 6.3 fusion.191
  309.6 27.1 %fusion.194 = bf16[2,512,6,64]{1,3,2,0:T(8,128)(2,1)} fusion(bf16[2,512,6,64]{1,3,2,0:T(8,128)(2,1)} %get-tuple-element.481, s32[]{:T(128)S(6)} %copy.130, bf16[1024,6,64]{0,2,1:T(8,128)(2,1)S(1)} %get-tuple-element.502, f32[6,512,1024]{2,1,0:T(8,128)} %fusion.191, f32[6,512,1024]{2,1,0:T(8,128)} %copy-done, ...), kind=kOutput, calls=%fused_computation.45.clone.1 | convolution fusion | flops 437653504 | bytes 52592644 | tf_op jit(solution)/shard_map/while/body/eval_jaxpr/hqk,khd->qhd/dot_general | solution.py:113
  336.7 29.5 %bitcast_add_fusion.6 = f32[1024,6,64]{0,2,1:T(8,128)} fusion(f32[1024,6,64]{0,2,1:T(8,128)} %get-tuple-element.479, f32[6,512,1024]{2,1,0:T(8,128)} %fusion.191, f32[6,512,1024]{2,1,0:T(8,128)} %copy-done, f32[6,512]{1,0:T(8,128)S(1)} %dynamic-slice_bitcast_fusion.2, pred[512,1024]{1,0:T(8,128)(4,1)S(1)} %fusion.193, pred[]{:T(512)S(6)} %compare.3, ...), kind=kOutput, calls=%fused_computation.41.clone.1 | convolution fusion | flops 438439936 | bytes 54951940 | tf_op jit(solution)/shard_map/while/body/eval_jaxpr/hqk,qhd->khd/dot_general | solution.py:118
  370.1 6.5 bitcast_add_fusion.7
  376.6 6.3 fusion.191
  382.9 27.3 %fusion.194 = bf16[2,512,6,64]{1,3,2,0:T(8,128)(2,1)} fusion(bf16[2,512,6,64]{1,3,2,0:T(8,128)(2,1)} %get-tuple-element.481, s32[]{:T(128)S(6)} %copy.130, bf16[1024,6,64]{0,2,1:T(8,128)(2,1)S(1)} %get-tuple-element.502, f32[6,512,1024]{2,1,0:T(8,128)} %fusion.191, f32[6,512,1024]{2,1,0:T(8,128)} %copy-done, ...), kind=kOutput, calls=%fused_computation.45.clone.1 | convolution fusion | flops 437653504 | bytes 52592644 | tf_op jit(solution)/shard_map/while/body/eval_jaxpr/hqk,khd->qhd/dot_general | solution.py:113
  410.2 29.8 %bitcast_add_fusion.6 = f32[1024,6,64]{0,2,1:T(8,128)} fusion(f32[1024,6,64]{0,2,1:T(8,128)} %get-tuple-element.479, f32[6,512,1024]{2,1,0:T(8,128)} %fusion.191, f32[6,512,1024]{2,1,0:T(8,128)} %copy-done, f32[6,512]{1,0:T(8,128)S(1)} %dynamic-slice_bitcast_fusion.2, pred[512,1024]{1,0:T(8,128)(4,1)S(1)} %fusion.193, pred[]{:T(512)S(6)} %compare.3, ...), kind=kOutput, calls=%fused_computation.41.clone.1 | convolution fusion | flops 438439936 | bytes 54951940 | tf_op jit(solution)/shard_map/while/body/eval_jaxpr/hqk,qhd->khd/dot_general | solution.py:118
  446.2 4.9 copy.103
  451.1 6.3 all_to_all.66
  466.3 5.1 fusion.105
  473.0 4.2 fusion.100
  479.3 38.3 %all-reduce.2 = f32[2,768]{1,0:T(2,128)S(1)} all-reduce(f32[2,768]{1,0:T(2,128)S(1)} %pad_maximum_fusion.8), channel_id=6, replica_groups=mesh['tok'=16,'hd'=2] {'tok','hd'}, use_global_device_ids=true, to_apply=%region_23.24.clone | all-reduce | flops 1536 | bytes 12288
  526.7 73.3 %reduce-scatter.12.cloned.1.call-done = f32[72,768]{1,0:T(8,128)} async-done(((f32[2304,768]{1,0:T(8,128)}), f32[72,768]{1,0:T(8,128)}) %reduce-scatter.12.cloned.1.call-update) | async-done | bytes 221200 | tf_op jit(solution)/shard_map/reduce_scatter | solution.py:270
  601.6 122.6 %reduce-scatter.8.cloned.1.call-done = f32[72,768]{1,0:T(8,128)} async-done(((f32[2304,768]{1,0:T(8,128)}), f32[72,768]{1,0:T(8,128)}) %reduce-scatter.8.cloned.1.call-update) | async-done | bytes 221200 | tf_op jit(solution)/shard_map/reduce_scatter | solution.py:268
  (252 shorter events, 136.7 us)
Async XLA Ops:
  7.2 66.5 %all-gather.7.cloned.1.call-start = ((), (), s32[]{:S(2)}) async-start(), calls=%async_computation.8 | async-start | bytes 3649536 | tf_op jit(solution)/shard_map/all_gather | solution.py:151
  7.9 151.9 %all-gather.9.cloned.1.call-start = ((), (), s32[]{:S(2)}) async-start(), calls=%async_computation.9 | async-start | bytes 1216512 | tf_op jit(solution)/shard_map/all_gather | solution.py:152
  8.6 182.5 %all-gather.11.cloned.1.call-start = ((), (), s32[]{:S(2)}) async-start(), calls=%async_computation.10 | async-start | bytes 3649536 | tf_op jit(solution)/shard_map/all_gather | solution.py:153
  9.4 238.7 %all-gather.13.cloned.1.call-start = ((), (), s32[]{:S(2)}) async-start(), calls=%async_computation.11 | async-start | bytes 1824768 | tf_op jit(solution)/shard_map/all_gather | solution.py:154
  10.0 513.7 %reduce-scatter.10.cloned.1.call-start = ((), (), s32[]{:S(2)}) async-start(), calls=%async_computation.13 | async-start | bytes 2433024 | tf_op jit(solution)/shard_map/reduce_scatter | solution.py:269
  17.1 56.6 %copy-start.34 = (f32[512]{0:T(512)}, f32[512]{0:T(512)S(1)}, u32[]{:S(2)}) copy-start(f32[512]{0:T(512)S(1)} %broadcast_multiply_fusion.6) | copy-start | bytes 6148
  18.6 51.2 %copy-start.40 = (f32[512]{0:T(512)}, f32[512]{0:T(512)S(1)}, u32[]{:S(2)}) copy-start(f32[512]{0:T(512)S(1)} %fusion.99) | copy-start | bytes 6148
  18.6 55.0 %copy-start.36 = (f32[512]{0:T(512)}, f32[512]{0:T(512)S(1)}, u32[]{:S(2)}) copy-start(f32[512]{0:T(512)S(1)} %fusion.118) | copy-start | bytes 6148
  65.5 8.2 %copy-start.30 = (f32[768]{0:T(1024)}, f32[768]{0:T(1024)S(1)}, u32[]{:S(2)}) copy-start(f32[768]{0:T(1024)S(1)} %get-tuple-element.201) | copy-start | bytes 9220
  66.5 7.2 copy-start.3
  155.0 4.8 copy-start.4
  155.0 4.8 copy-start.32
  159.8 31.4 %copy-start.42 = (f32[768]{0:T(1024)S(1)}, f32[768]{0:T(1024)}, u32[]{:S(2)}) copy-start(f32[768]{0:T(1024)} %get-tuple-element.200) | copy-start | bytes 9220
  191.1 57.0 %copy-start.8 = (bf16[512,768]{1,0:T(8,128)(2,1)S(1)}, bf16[512,768]{1,0:T(8,128)(2,1)}, u32[]{:S(2)}) copy-start(bf16[512,768]{1,0:T(8,128)(2,1)} %param.19) | copy-start | bytes 2359300
  248.1 9.0 %copy-start.15 = (f32[512,2304]{1,0:T(8,128)S(1)}, f32[512,2304]{1,0:T(8,128)}, u32[]{:S(2)}) copy-start(f32[512,2304]{1,0:T(8,128)} %fusion.128) | copy-start | bytes 14155780
  257.1 3.7 copy-start.44
  258.7 4.9 copy-start.20
  268.8 256.3 %reduce-scatter.14.cloned.1.call-start = ((), (), s32[]{:S(2)}) async-start(), calls=%async_computation.15 | async-start | bytes 3649536
  273.2 326.7 %reduce-scatter.12.cloned.1.call-start = ((), (), s32[]{:S(2)}) async-start(), calls=%async_computation.14 | async-start | bytes 7299072 | tf_op jit(solution)/shard_map/reduce_scatter | solution.py:270
  280.6 443.6 %reduce-scatter.8.cloned.1.call-start = ((), (), s32[]{:S(2)}) async-start(), calls=%async_computation.12 | async-start | bytes 7299072 | tf_op jit(solution)/shard_map/reduce_scatter | solution.py:268
  298.3 5.0 copy-start
  370.1 6.5 copy-start
  440.2 2.6 copy-start.19
  462.4 2.7 copy-start.23
  473.0 4.3 copy-start.41
  477.3 41.0 %copy-start.2 = (f32[512,768]{1,0:T(8,128)S(1)}, f32[512,768]{1,0:T(8,128)}, u32[]{:S(2)}) copy-start(f32[512,768]{1,0:T(8,128)} %copy-done.1) | copy-start | bytes 4718596
  477.3 40.9 %copy-start.9 = (bf16[512,768]{1,0:T(8,128)(2,1)S(1)}, bf16[512,768]{1,0:T(8,128)(2,1)}, u32[]{:S(2)}) copy-start(bf16[512,768]{1,0:T(8,128)(2,1)} %param.19) | copy-start | bytes 2359300
  477.3 40.9 %copy-start.39 = (f32[512]{0:T(512)S(1)}, f32[512]{0:T(512)}, u32[]{:S(2)}) copy-start(f32[512]{0:T(512)} %copy-done.38) | copy-start | bytes 6148
  518.2 3.2 copy-start.12
  518.2 3.2 copy-start.14
  518.3 3.2 copy-start.33
  518.3 3.2 copy-start.45
  (25 other events, 36.2 us)
Sparse Core Ops, SparseCore 0:
  10.9 62.7 all-gather.6
  76.6 52.7 all-gather.8
  132.2 58.8 all-gather.10
  193.8 54.2 all-gather.12
  269.0 98.8 reduce-scatter.9
  373.2 102.4 reduce-scatter.13
  481.3 118.5 reduce-scatter.11
  605.6 118.4 reduce-scatter.7
where the time goes:
time: 742 us; the launch traced here: 733 us
  waiting for transfers between devices  279 us (38%)
  matrix products  208 us (28%)
  blocking collectives  108 us (15%)
  local copies, waits for them, and re-layouts  72.7 us (10%)
  other arithmetic  47 us (6%)
  between operations  15.7 us (2%)
    reduce_scatter x1, waiting for transfers between devices, per_device(): lax.psum_scatter(qkv_term, ('tok', 'hd'), scatter_dimension=0, tiled=True)  123 us
    reduce_scatter x1, waiting for transfers between devices, per_device(): lax.psum_scatter(in_term, ('tok', 'hd'), scatter_dimension=0, tiled=True)  73.3 us
    dot_general x2, matrix products, one_block(): jnp.einsum('hqk,qhd->khd', grad_scores, query_block, preferred_element_ty...  59.3 us
    dot_general x2, matrix products, one_block(): jnp.einsum('hqk,khd->qhd', grad_scores, keys, preferred_element_type=jnp....  54.3 us
    all_gather x1, waiting for transfers between devices, per_device(): lax.all_gather(w_down, ('tok', 'hd'), axis=0, tiled=True)  50.2 us
    all_gather x1, blocking collectives, per_device(): lax.all_gather(norm_gains, ('tok', 'hd'), axis=1, tiled=True)  43.4 us
    unnamed x2, blocking collectives  40.3 us
    all_gather x1, waiting for transfers between devices, per_device(): lax.all_gather(w_in, ('tok', 'hd'), axis=0, tiled=True)  27.4 us
  transfers between devices with their start and end apart: 8, of which 5 were waited for; matrix products, arithmetic and copies ran while one was open for 40% of the time, Pallas kernels for 0%

commit v1 on v0

--- a/solution.py
+++ b/solution.py
@@ -9,6 +9,18 @@
 EPS = 1e-05
 THETA = 160000.0
 NEG = -1e30
+
+
+def treat_edge_in(local_block):
+    extent = lax.axis_size(("tok", "hd"))
+    found_now = lax.all_to_all(
+        jnp.tile(local_block, [extent if h == 0 else 1 for h in range(local_block.ndim)]),
+        ("tok", "hd"),
+        split_axis=0,
+        tiled=True,
+        concat_axis=0,
+    )
+    return found_now
 
 
 def layer_norm(row_values, gain):
@@ -151,7 +163,7 @@
         lax.all_gather(w_qkv, ("tok", "hd"), axis=0, tiled=True),
         lax.all_gather(w_attn_out, ("tok", "hd"), axis=0, tiled=True),
         lax.all_gather(w_in, ("tok", "hd"), axis=0, tiled=True),
-        lax.all_gather(w_down, ("tok", "hd"), axis=0, tiled=True),
+        treat_edge_in(w_down),
         lax.all_gather(norm_gains, ("tok", "hd"), axis=1, tiled=True),
     )
     full_qkv, full_attn_out, full_in, full_down, full_gains = gathered

time: 742 us -> 742 us (level)
  waiting for transfers between devices: 279 us -> 234 us
  blocking collectives: 108 us -> 131 us
  matrix products: 208 us -> 226 us
    reduce_scatter x1, waiting for transfers between devices: 73.3 us -> 27.5 us  [per_device(): lax.psum_scatter(in_term, ('tok', 'hd'), scatter_dimension=0, tiled=True)]
    unnamed x2, blocking collectives: 40.3 us -> 63.4 us
    dot_general x4, matrix products: 8.51 us -> 17.6 us  [block_scores(): jnp.einsum('qhd,khd->hqk', query_block, keys, preferred_element_type=jnp....]
    dot_general x2, matrix products: 11.5 us -> 19 us  [one_block(): jnp.einsum('hqk,qhd->khd', probs_low, grad_block, preferred_element_type=...]
    unnamed x98 -> x100, local copies, waits for them, and re-layouts: 22.2 us -> 21 us
  transfers between devices with their start and end apart: 8 -> 9, of which waited for: 5 -> 5; matrix products, arithmetic and copies ran while one was open for 40% -> 43% of each run, Pallas kernels for 0% -> 0%
where the time goes in v1:
time: 742 us; the launch traced here: 734 us
  waiting for transfers between devices  234 us (32%)
  matrix products  226 us (30%)
  blocking collectives  131 us (18%)
  local copies, waits for them, and re-layouts  74.4 us (10%)
  other arithmetic  44.7 us (6%)
  between operations  15.9 us (2%)
    reduce_scatter x1, waiting for transfers between devices, per_device(): lax.psum_scatter(qkv_term, ('tok', 'hd'), scatter_dimension=0, tiled=True)  123 us
    unnamed x2, blocking collectives  63.4 us
    dot_general x2, matrix products, one_block(): jnp.einsum('hqk,qhd->khd', grad_scores, query_block, preferred_element_ty...  59.4 us
    dot_general x2, matrix products, one_block(): jnp.einsum('hqk,khd->qhd', grad_scores, keys, preferred_element_type=jnp....  54.1 us
    all_gather x1, waiting for transfers between devices, per_device(): lax.all_gather(w_down, ('tok', 'hd'), axis=0, tiled=True)  50.2 us
    all_gather x1, blocking collectives, per_device(): lax.all_gather(norm_gains, ('tok', 'hd'), axis=1, tiled=True)  43.6 us
    all_gather x1, waiting for transfers between devices, per_device(): lax.all_gather(w_in, ('tok', 'hd'), axis=0, tiled=True)  27.8 us
    reduce_scatter x1, waiting for transfers between devices, per_device(): lax.psum_scatter(in_term, ('tok', 'hd'), scatter_dimension=0, tiled=True)  27.5 us
  transfers between devices with their start and end apart: 9, of which 5 were waited for; matrix products, arithmetic and copies ran while one was open for 43% of the time, Pallas kernels for 0%

profile of v1, /device:TPU:0, one launch (start us, length us, event | category | flops | bytes accessed | tf_op | source)
XLA Modules:
  0.0 733.6 jit_solution(16457114319937073787)
XLA Ops:
  12.9 43.6 %all-gather.1 = bf16[32,24,2]{1,2,0:T(2,128)(2,1)S(1)} all-gather(bf16[1,24,2]{1,2,0:T(2,128)(2,1)} %bitcast.177), channel_id=1, replica_groups=mesh['tok'=16,'hd'=2] {'tok','hd'}, dimensions={0}, use_global_device_ids=true | all-gather | bytes 3168 | tf_op jit(solution)/shard_map/all_gather | solution.py:167
  105.3 5.8 all_to_all.72
  112.6 25.3 %while.27 = (s32[]{:T(128)}, bf16[2,512,6,64]{1,3,2,0:T(8,128)(2,1)S(1)}, f32[2,6,512]{2,1,0:T(8,128)S(1)}, s32[2]{0:T(128)S(1)}, s32[1024]{0:T(1024)S(1)}, /*in...) while((s32[]{:T(128)}, ...), condition=%wide.region_7.8_spmd, body=%wide.region_4.7_spmd.sunk | while | flops 845870592 | bytes 42341068 | solution.py:101
  120.8 4.4 fusion.180
  133.4 4.4 fusion.180
  147.0 5.9 all_to_all.73
  163.3 27.8 %all-gather.11.cloned.1.call-done = bf16[2304,768]{1,0:T(8,128)(2,1)} async-done(((bf16[72,768]{1,0:T(8,128)(2,1)}), bf16[2304,768]{1,0:T(8,128)(2,1)}) %all-gather.11.cloned.1.call-update) | async-done | bytes 3538960 | tf_op jit(solution)/shard_map/all_gather | solution.py:165
  191.1 6.8 fusion.128
  197.9 50.2 %all-gather.13.cloned.1.call-done = bf16[768,1152]{1,0:T(8,128)(2,1)} async-done(((bf16[24,1152]{1,0:T(8,128)(2,1)}), bf16[768,1152]{1,0:T(8,128)(2,1)}) %all-gather.13.cloned.1.call-update) | async-done | bytes 1769488 | tf_op jit(solution)/shard_map/all_gather | solution.py:216
  248.0 9.0 %add_convert_fusion = (bf16[512,1152]{1,0:T(8,128)(2,1)S(1)}, f32[512,1152]{1,0:T(8,128)S(1)}, f32[512,1152]{1,0:T(8,128)S(1)}) fusion(f32[512,2304]{1,0:T(8,128)} %fusion.128, bf16[768,1152]{1,0:T(8,128)(2,1)} %all-gather.13.cloned.1.call-done, bf16[512,768]{1,0:T(8,128)(2,1)S(1)} %copy-done.7, f32[512]{0:T(512)S(1)} %copy-done.32), kind=kOutput, calls=%fused_computation.82 | convolution fusion | flops 950206464 | bytes 13174784 | tf_op jit(solution)/shard_map/dot_general | solution.py:67
  268.8 4.3 fusion.107
  273.3 7.2 fusion.103
  283.8 4.4 all_to_all.74
  294.2 162.8 %while.28 = (s32[]{:T(128)}, f32[1024,6,64]{0,2,1:T(8,128)}, f32[1024,6,64]{0,2,1:T(8,128)}, bf16[2,512,6,64]{1,3,2,0:T(8,128)(2,1)}, s32[2]{0:T(128)S(1)}, /*in...) while((s32[]{:T(128)}, f32[1024,6,64]{0,2,1:T(8,128)}, ...), condition=%wide.region_14.15_spmd.clone, body=%wide.region_12.14_spmd.clone.sunk | while | flops 2100044288 | bytes 155440416 | solution.py:142
  296.6 6.4 fusion.192
  303.0 6.3 fusion.191
  309.3 29.6 %bitcast_add_fusion.6 = f32[1024,6,64]{0,2,1:T(8,128)} fusion(f32[1024,6,64]{0,2,1:T(8,128)} %get-tuple-element.479, f32[6,512,1024]{2,1,0:T(8,128)} %fusion.191, f32[6,512,1024]{2,1,0:T(8,128)} %fusion.192, f32[6,512]{1,0:T(8,128)S(1)} %dynamic-slice_bitcast_fusion.2, pred[512,1024]{1,0:T(8,128)(4,1)S(1)} %fusion.193, pred[]{:T(512)S(6)} %compare.3, ...), kind=kOutput, calls=%fused_computation.41.clone.1 | convolution fusion | flops 438439936 | bytes 54951940 | tf_op jit(solution)/shard_map/while/body/eval_jaxpr/hqk,qhd->khd/dot_general | solution.py:130
  338.9 26.9 %fusion.194 = bf16[2,512,6,64]{1,3,2,0:T(8,128)(2,1)} fusion(bf16[2,512,6,64]{1,3,2,0:T(8,128)(2,1)} %get-tuple-element.481, s32[]{:T(128)} %get-tuple-element.478, bf16[1024,6,64]{0,2,1:T(8,128)(2,1)S(1)} %get-tuple-element.502, f32[6,512,1024]{2,1,0:T(8,128)} %fusion.191, f32[6,512,1024]{2,1,0:T(8,128)} %fusion.192, ...), kind=kOutput, calls=%fused_computation.45.clone.1 | convolution fusion | flops 437653504 | bytes 52593152 | tf_op jit(solution)/shard_map/while/body/eval_jaxpr/hqk,khd->qhd/dot_general | solution.py:125
  365.8 9.3 %bitcast_add_fusion.7 = f32[1024,6,64]{0,2,1:T(8,128)} fusion(f32[1024,6,64]{0,2,1:T(8,128)} %get-tuple-element.480, f32[6,512,1024]{2,1,0:T(8,128)} %fusion.192, f32[6,512]{1,0:T(8,128)S(1)} %dynamic-slice_bitcast_fusion.2, pred[512,1024]{1,0:T(8,128)(4,1)S(1)} %fusion.193, pred[]{:T(512)S(6)} %compare.3, ...), kind=kOutput, calls=%fused_computation.40.clone.1 | convolution fusion | flops 416022528 | bytes 16658437 | tf_op jit(solution)/shard_map/while/body/eval_jaxpr/hqk,qhd->khd/dot_general | solution.py:135
  377.3 6.4 fusion.192
  383.7 6.3 fusion.191
  390.0 29.8 %bitcast_add_fusion.6 = f32[1024,6,64]{0,2,1:T(8,128)} fusion(f32[1024,6,64]{0,2,1:T(8,128)} %get-tuple-element.479, f32[6,512,1024]{2,1,0:T(8,128)} %fusion.191, f32[6,512,1024]{2,1,0:T(8,128)} %fusion.192, f32[6,512]{1,0:T(8,128)S(1)} %dynamic-slice_bitcast_fusion.2, pred[512,1024]{1,0:T(8,128)(4,1)S(1)} %fusion.193, pred[]{:T(512)S(6)} %compare.3, ...), kind=kOutput, calls=%fused_computation.41.clone.1 | convolution fusion | flops 438439936 | bytes 54951940 | tf_op jit(solution)/shard_map/while/body/eval_jaxpr/hqk,qhd->khd/dot_general | solution.py:130
  419.8 27.3 %fusion.194 = bf16[2,512,6,64]{1,3,2,0:T(8,128)(2,1)} fusion(bf16[2,512,6,64]{1,3,2,0:T(8,128)(2,1)} %get-tuple-element.481, s32[]{:T(128)} %get-tuple-element.478, bf16[1024,6,64]{0,2,1:T(8,128)(2,1)S(1)} %get-tuple-element.502, f32[6,512,1024]{2,1,0:T(8,128)} %fusion.191, f32[6,512,1024]{2,1,0:T(8,128)} %fusion.192, ...), kind=kOutput, calls=%fused_computation.45.clone.1 | convolution fusion | flops 437653504 | bytes 52593152 | tf_op jit(solution)/shard_map/while/body/eval_jaxpr/hqk,khd->qhd/dot_general | solution.py:125
  447.1 9.7 %bitcast_add_fusion.7 = f32[1024,6,64]{0,2,1:T(8,128)} fusion(f32[1024,6,64]{0,2,1:T(8,128)} %get-tuple-element.480, f32[6,512,1024]{2,1,0:T(8,128)} %fusion.192, f32[6,512]{1,0:T(8,128)S(1)} %dynamic-slice_bitcast_fusion.2, pred[512,1024]{1,0:T(8,128)(4,1)S(1)} %fusion.193, pred[]{:T(512)S(6)} %compare.3, ...), kind=kOutput, calls=%fused_computation.40.clone.1 | convolution fusion | flops 416022528 | bytes 16658437 | tf_op jit(solution)/shard_map/while/body/eval_jaxpr/hqk,qhd->khd/dot_general | solution.py:135
  462.8 4.9 copy.103
  467.7 6.3 all_to_all.75
  482.9 5.1 fusion.105
  494.0 4.4 fusion.100
  500.3 61.5 %all-reduce.2 = f32[2,768]{1,0:T(2,128)S(1)} all-reduce(f32[2,768]{1,0:T(2,128)S(1)} %pad_maximum_fusion.8), channel_id=6, replica_groups=mesh['tok'=16,'hd'=2] {'tok','hd'}, use_global_device_ids=true, to_apply=%region_23.24.clone | all-reduce | flops 1536 | bytes 12288
  565.5 4.4 add_convert_fusion.2
  573.0 27.5 %reduce-scatter.12.cloned.1.call-done = f32[72,768]{1,0:T(8,128)} async-done(((f32[2304,768]{1,0:T(8,128)}), f32[72,768]{1,0:T(8,128)}) %reduce-scatter.12.cloned.1.call-update) | async-done | bytes 221200 | tf_op jit(solution)/shard_map/reduce_scatter | solution.py:282
  602.2 122.6 %reduce-scatter.8.cloned.1.call-done = f32[72,768]{1,0:T(8,128)} async-done(((f32[2304,768]{1,0:T(8,128)}), f32[72,768]{1,0:T(8,128)}) %reduce-scatter.8.cloned.1.call-update) | async-done | bytes 221200 | tf_op jit(solution)/shard_map/reduce_scatter | solution.py:280
  (253 shorter events, 146.2 us)
Async XLA Ops:
  7.2 54.4 %copy-start.45 = (u32[32]{0:T(128)S(1)}, u32[32]{0:T(128)}, u32[]{:S(2)}) copy-start(u32[32]{0:T(128)} %constant.163) | copy-start | bytes 388
  7.2 66.5 %all-gather.7.cloned.1.call-start = ((), (), s32[]{:S(2)}) async-start(), calls=%async_computation.9 | async-start | bytes 3649536 | tf_op jit(solution)/shard_map/all_gather | solution.py:163
  7.9 151.4 %all-gather.9.cloned.1.call-start = ((), (), s32[]{:S(2)}) async-start(), calls=%async_computation.10 | async-start | bytes 1216512 | tf_op jit(solution)/shard_map/all_gather | solution.py:164
  8.7 182.4 %all-gather.11.cloned.1.call-start = ((), (), s32[]{:S(2)}) async-start(), calls=%async_computation.11 | async-start | bytes 3649536 | tf_op jit(solution)/shard_map/all_gather | solution.py:165
  9.4 238.6 %all-gather.13.cloned.1.call-start = ((), (), s32[]{:S(2)}) async-start(), calls=%async_computation.12 | async-start | bytes 1824768 | tf_op jit(solution)/shard_map/all_gather | solution.py:216
  10.0 560.0 %reduce-scatter.10.cloned.1.call-start = ((), (), s32[]{:S(2)}) async-start(), calls=%async_computation.14 | async-start | bytes 2433024 | tf_op jit(solution)/shard_map/reduce_scatter | solution.py:281
  11.4 62.3 %copy-start.34 = (f32[512]{0:T(512)}, f32[512]{0:T(512)S(1)}, u32[]{:S(2)}) copy-start(f32[512]{0:T(512)S(1)} %broadcast_multiply_fusion.6) | copy-start | bytes 6148
  12.9 43.6 %copy-start.40 = (f32[512]{0:T(512)}, f32[512]{0:T(512)S(1)}, u32[]{:S(2)}) copy-start(f32[512]{0:T(512)S(1)} %fusion.99) | copy-start | bytes 6148
  12.9 60.8 %copy-start.36 = (f32[512]{0:T(512)}, f32[512]{0:T(512)S(1)}, u32[]{:S(2)}) copy-start(f32[512]{0:T(512)S(1)} %fusion.118) | copy-start | bytes 6148
  57.2 16.5 %copy-start.30 = (f32[768]{0:T(1024)}, f32[768]{0:T(1024)S(1)}, u32[]{:S(2)}) copy-start(f32[768]{0:T(1024)S(1)} %get-tuple-element.201) | copy-start | bytes 9220
  61.0 3.4 copy-start.20
  63.0 10.7 %copy-start.2 = (bf16[512,768]{1,0:T(8,128)(2,1)S(1)}, bf16[512,768]{1,0:T(8,128)(2,1)}, u32[]{:S(2)}) copy-start(bf16[512,768]{1,0:T(8,128)(2,1)} %param.13) | copy-start | bytes 2359300
  154.5 4.8 copy-start.3
  154.5 4.8 copy-start.32
  159.3 31.8 %copy-start.42 = (f32[768]{0:T(1024)S(1)}, f32[768]{0:T(1024)}, u32[]{:S(2)}) copy-start(f32[768]{0:T(1024)} %get-tuple-element.200) | copy-start | bytes 9220
  191.1 57.0 %copy-start.7 = (bf16[512,768]{1,0:T(8,128)(2,1)S(1)}, bf16[512,768]{1,0:T(8,128)(2,1)}, u32[]{:S(2)}) copy-start(bf16[512,768]{1,0:T(8,128)(2,1)} %param.19) | copy-start | bytes 2359300
  248.0 9.0 %copy-start.12 = (f32[512,2304]{1,0:T(8,128)S(1)}, f32[512,2304]{1,0:T(8,128)}, u32[]{:S(2)}) copy-start(f32[512,2304]{1,0:T(8,128)} %fusion.128) | copy-start | bytes 14155780
  257.1 3.7 copy-start.44
  258.7 4.9 copy-start.19
  268.8 302.7 %reduce-scatter.14.cloned.1.call-start = ((), (), s32[]{:S(2)}) async-start(), calls=%async_computation.16 | async-start | bytes 3649536
  273.2 327.4 %reduce-scatter.12.cloned.1.call-start = ((), (), s32[]{:S(2)}) async-start(), calls=%async_computation.15 | async-start | bytes 7299072 | tf_op jit(solution)/shard_map/reduce_scatter | solution.py:282
  280.5 444.2 %reduce-scatter.8.cloned.1.call-start = ((), (), s32[]{:S(2)}) async-start(), calls=%async_computation.13 | async-start | bytes 7299072 | tf_op jit(solution)/shard_map/reduce_scatter | solution.py:280
  296.6 6.4 copy-start.6
  377.3 6.4 copy-start.6
  488.8 5.1 copy-start.23
  488.8 5.1 copy-start.25
  488.8 5.1 copy-start.27
  490.2 75.4 %all-to-all-start.2 = ((bf16[32,24,1152]{2,1,0:T(8,128)(2,1)}), bf16[32,24,1152]{2,1,0:T(8,128)(2,1)}, u32[]{:S(2)}, u32[]{:S(2)}) async-start(bf16[32,24,1152]{2,1,0:T(8,128)(2,1)} %tile.2), calls=%async_computation.2 | async-start | bytes 3538944 | tf_op jit(solution)/shard_map/all_to_all | solution.py:16
  494.0 4.4 copy-start.41
  498.3 64.2 %copy-start.1 = (f32[512,768]{1,0:T(8,128)S(1)}, f32[512,768]{1,0:T(8,128)}, u32[]{:S(2)}) copy-start(f32[512,768]{1,0:T(8,128)} %copy-done) | copy-start | bytes 4718596
  498.3 64.2 %copy-start.8 = (bf16[512,768]{1,0:T(8,128)(2,1)S(1)}, bf16[512,768]{1,0:T(8,128)(2,1)}, u32[]{:S(2)}) copy-start(bf16[512,768]{1,0:T(8,128)(2,1)} %param.19) | copy-start | bytes 2359300
  498.4 64.2 %copy-start.39 = (f32[512]{0:T(512)S(1)}, f32[512]{0:T(512)}, u32[]{:S(2)}) copy-start(f32[512]{0:T(512)} %copy-done.38) | copy-start | bytes 6148
  (25 other events, 42.3 us)
Sparse Core Ops, SparseCore 0:
  10.9 62.7 all-gather.6
  76.6 52.8 all-gather.8
  132.3 58.6 all-gather.10
  193.8 54.2 all-gather.12
  268.9 98.8 reduce-scatter.9
  373.1 102.4 reduce-scatter.13
  481.3 119.1 reduce-scatter.11
  606.2 118.4 reduce-scatter.7
